TPU v7x, 32 devices: a whole 2x2x4 slice. The times are simulated.
32 devices in a mesh: expert: 8 (over z, x), dp: 4 (over y, core).
Axes of the slice: x: 2, y: 2, z: 4, core: 2. Of those that a mesh axis runs over, the one named last changes fastest.
Arguments:
- enc_state: bfloat16 [4, 8, 256, 1024], P('dp', 'expert'), may hold values from -6 to 6
- baseline: bfloat16 [4, 8, 256, 1024], P('dp', 'expert'), may hold values from -6 to 6
- enc_keys: bfloat16 [4, 8, 256, 1024], P('dp', 'expert'), may hold values from -4 to 4
- dec_queries: bfloat16 [4, 8, 128, 1024], P('dp', 'expert'), may hold values from -200 to 200
- out_mult: bfloat16 [4, 8, 128, 1024], P('dp', 'expert'), may hold values from -6 to 6
- doc_lengths: int32 [4, 8], P('dp', 'expert'), may hold values from 128 to 256, as said below
- expert_ids: int32 [4, 8, 256], P('dp', 'expert'), may hold values from 0 to 15
- slot_ids: int32 [4, 8, 256], P('dp', 'expert'), may hold values from 0 to 31, as said below
- gate_prob: float32 [4, 8, 256], P('dp', 'expert'), may hold values from 0.2 to 1
- norm_gain: float32 [1024], replicated, may hold values from 0.5 to 2
- w_in: bfloat16 [16, 1024, 2816], P('expert', None, 'dp'), may hold values from -0.1875 to 0.1875
- w_out_t: bfloat16 [16, 1024, 2816], P('expert', None, 'dp'), may hold values from -0.109375 to 0.109375
- w_value: bfloat16 [1024, 1024], replicated, may hold values from -0.1875 to 0.1875
Outputs:
- enc_mult: bfloat16 [4, 8, 256, 1024], P('dp', 'expert')
Inputs may be any that keep to these rules, and one draw needn't show every extreme that they name: `slot_ids`: within one document no two tokens share an expert and a slot, and every token has a slot; one expert has all 32 slots used in every document. `doc_lengths`: some document has all 256 tokens.
All inputs are finite; a program needn't handle non-finite values.
Results may differ from a plain program's by a relative error of at most 0.0069.
Values may be sent and summed in bfloat16 or wider, within the bound.
A program may use at most 128 MiB of HBM per device.

v0:
```python
import math
import jax
import jax.numpy as jnp
from jax import lax
from jax.sharding import PartitionSpec as P

HEADS = 16
HEAD_DIM = 64


def rescale(pre_act, base_act):
    upper_part = jnp.maximum(jnp.maximum(pre_act, base_act), 0.0)
    lower_part = jnp.maximum(-jnp.minimum(pre_act, base_act), 0.0)
    return upper_part / (upper_part + lower_part + jnp.where(upper_part > 0.0, 0.0, 1.0))


def attend(query_rows, key_rows, mult_rows, length, w_value):
    enc_len = key_rows.shape[0]
    dec_len = query_rows.shape[0]
    queries = query_rows.reshape(dec_len, HEADS, HEAD_DIM)
    keys = key_rows.reshape(enc_len, HEADS, HEAD_DIM)
    mults = mult_rows.reshape(dec_len, HEADS, HEAD_DIM)
    scores = jnp.einsum("qhd,khd->hqk", queries, keys, preferred_element_type=jnp.float32) * (
        1.0 / math.sqrt(HEAD_DIM)
    )
    valid = jnp.arange(enc_len, dtype=jnp.int32) < length
    scores = jnp.where(valid[None, None, :], scores, -jnp.inf)
    top_score = jnp.max(scores, axis=-1, keepdims=True)
    expo = jnp.exp(scores - top_score)
    attn = (expo / jnp.sum(expo, axis=-1, keepdims=True)).astype(jnp.bfloat16)
    value_mult = jnp.einsum("hqk,qhd->khd", attn, mults, preferred_element_type=jnp.float32).astype(
        jnp.bfloat16
    )
    return lax.dot_general(
        value_mult.reshape(enc_len, HEADS * HEAD_DIM),
        w_value,
        (((1,), (1,)), ((), ())),
        preferred_element_type=jnp.float32,
    )


def expert_terms(rows_in, rows_base, rows_mult, part_in, part_out):
    pre_act = jnp.einsum("erd,edf->erf", rows_in, part_in, preferred_element_type=jnp.float32)
    base_act = jnp.einsum("erd,edf->erf", rows_base, part_in, preferred_element_type=jnp.float32)
    hidden_mult = jnp.einsum(
        "erd,edf->erf", rows_mult, part_out, preferred_element_type=jnp.float32
    )
    act_mult = (rescale(pre_act, base_act) * hidden_mult).astype(jnp.bfloat16)
    return jnp.einsum("erf,edf->erd", act_mult, part_in, preferred_element_type=jnp.float32)


def body(
    enc_state,
    baseline,
    enc_keys,
    dec_queries,
    out_mult,
    doc_lengths,
    expert_ids,
    slot_ids,
    gate_prob,
    norm_gain,
    w_in,
    w_out_t,
    w_value,
):
    enc_len = enc_state.shape[2]
    feature_width = enc_state.shape[3]
    local_experts = w_in.shape[0]
    n_experts = local_experts * lax.axis_size("expert")
    capacity = max(2, 2 * enc_len // n_experts)
    tokens = enc_state[0, 0].astype(jnp.float32)
    row_scale = norm_gain * lax.rsqrt(jnp.mean(tokens * tokens, axis=-1, keepdims=True) + 1e-06)
    inputs = (tokens * row_scale).astype(jnp.bfloat16)
    base_inputs = (baseline[0, 0].astype(jnp.float32) * row_scale).astype(jnp.bfloat16)
    flat_slot = expert_ids[0, 0] * capacity + slot_ids[0, 0]
    onehot = (
        flat_slot[None, :] == jnp.arange(n_experts * capacity, dtype=jnp.int32)[:, None]
    ).astype(jnp.bfloat16)

    def dispatch(values):
        placed = jnp.dot(onehot, values, preferred_element_type=jnp.float32).astype(jnp.bfloat16)
        return placed.reshape(n_experts, capacity, feature_width)

    layer_mult = attend(
        dec_queries[0, 0], enc_keys[0, 0], out_mult[0, 0], doc_lengths[0, 0], w_value
    )
    scaled_mult = (gate_prob[0, 0][:, None] * layer_mult).astype(jnp.bfloat16)
    sent_in, sent_base, sent_mult = (
        lax.all_to_all(dispatch(inputs), "expert", split_axis=0, concat_axis=1, tiled=True),
        lax.all_to_all(dispatch(base_inputs), "expert", split_axis=0, concat_axis=1, tiled=True),
        lax.all_to_all(dispatch(scaled_mult), "expert", split_axis=0, concat_axis=1, tiled=True),
    )
    slot_mult = expert_terms(
        sent_in,
        sent_base,
        sent_mult,
        lax.all_gather(w_in, "dp", axis=2, tiled=True),
        lax.all_gather(w_out_t, "dp", axis=2, tiled=True),
    )
    returned = lax.all_to_all(
        slot_mult.astype(jnp.bfloat16), "expert", split_axis=1, concat_axis=0, tiled=True
    )
    per_token = lax.dot_general(
        onehot,
        returned.reshape(n_experts * capacity, feature_width),
        (((0,), (0,)), ((), ())),
        preferred_element_type=jnp.float32,
    )
    result = (layer_mult + row_scale * per_token).astype(jnp.bfloat16)
    return result[None, None]


def solution(mesh):
    in_specs = (
        P("dp", "expert", None, None),
        P("dp", "expert", None, None),
        P("dp", "expert", None, None),
        P("dp", "expert", None, None),
        P("dp", "expert", None, None),
        P("dp", "expert"),
        P("dp", "expert", None),
        P("dp", "expert", None),
        P("dp", "expert", None),
        P(),
        P("expert", None, "dp"),
        P("expert", None, "dp"),
        P(),
    )
    out_specs = P("dp", "expert", None, None)
    return jax.shard_map(body, mesh=mesh, in_specs=in_specs, out_specs=out_specs, check_vma=False)
```

profile of v0, /device:TPU:0, one launch (start us, length us, event | category | flops | bytes accessed | tf_op | source)
XLA Modules:
  0.0 230.6 jit_solution(66276424766294604)
XLA Ops:
  6.5 0.0 copy-start
  6.5 0.0 copy-start.4
  6.5 0.0 copy-start.8
  6.5 0.0 copy-start.9
  6.5 0.0 all-gather.3.cloned.1.call-start
  6.6 0.7 all-gather.3.cloned.1.call-update
  7.3 0.0 copy-start.5
  7.3 0.0 all-gather.5.cloned.1.call-start
  7.3 0.7 all-gather.5.cloned.1.call-update
  8.0 0.0 copy-done.4
  8.1 0.2 fusion.5
  8.2 0.0 copy-done.8
  8.3 0.0 copy-done.9
  8.3 0.0 copy-done.6
  8.3 2.6 %convolution_convert_fusion.1 = bf16[512,1024]{1,0:T(8,128)(2,1)} fusion(bf16[1,1,256,1024]{3,2,1,0:T(8,128)(2,1)} %param.14, f32[256]{0:T(256)S(1)} %add_rsqrt_fusion, f32[1024]{0:T(1024)S(1)} %copy-done.6, s32[256]{0:T(256)S(1)} %bitcast.71), kind=kOutput, calls=%fused_computation.10 | convolution fusion | flops 270139392 | bytes 1579008 | tf_op jit(solution)/shard_map/dot_general | solution.py:82
  10.9 7.3 %all-to-all-start.1 = ((bf16[16,32,1024]{2,1,0:T(8,128)(2,1)}), bf16[16,32,1024]{2,1,0:T(8,128)(2,1)S(1)}, u32[]{:S(2)}, u32[]{:S(2)}) async-start(bf16[16,32,1024]{2,1,0:T(8,128)(2,1)} %bitcast.66), calls=%async_computation.1 | async-start | bytes 2097152 | tf_op jit(solution)/shard_map/all_to_all | solution.py:91
  18.2 2.6 %convolution_convert_fusion.2 = bf16[512,1024]{1,0:T(8,128)(2,1)} fusion(bf16[1,1,256,1024]{3,2,1,0:T(8,128)(2,1)} %param.13, f32[256]{0:T(256)S(1)} %add_rsqrt_fusion, f32[1024]{0:T(1024)S(1)} %copy-done.6, s32[256]{0:T(256)S(1)} %bitcast.72), kind=kOutput, calls=%fused_computation.11 | convolution fusion | flops 270139392 | bytes 1579008 | tf_op jit(solution)/shard_map/dot_general | solution.py:82
  20.8 23.1 %all-to-all-done.1 = bf16[16,32,1024]{2,1,0:T(8,128)(2,1)S(1)} async-done(((bf16[16,32,1024]{2,1,0:T(8,128)(2,1)}), bf16[16,32,1024]{2,1,0:T(8,128)(2,1)S(1)}, u32[]{:S(2)}, u32[]{:S(2)}) %all-to-all-start.1) | async-done | bytes 1048608 | tf_op jit(solution)/shard_map/all_to_all | solution.py:91
  44.0 4.2 %all-to-all-start = ((bf16[16,32,1024]{2,1,0:T(8,128)(2,1)}), bf16[16,32,1024]{2,1,0:T(8,128)(2,1)}, u32[]{:S(2)}, u32[]{:S(2)}) async-start(bf16[16,32,1024]{2,1,0:T(8,128)(2,1)} %bitcast.62), calls=%async_computation | async-start | bytes 2097152 | tf_op jit(solution)/shard_map/all_to_all | solution.py:90
  48.9 0.0 copy-done.5
  48.9 0.8 copy.39
  49.7 1.1 copy.41
  50.8 2.0 copy.40
  52.9 3.2 %fusion.28 = (f32[16,128]{1,0:T(8,128)S(1)}, f32[16,128,256]{2,1,0:T(8,128)}) fusion(pred[256]{0:T(512)(128)(4,1)S(1)} %iota_compare_fusion.5, bf16[128,16,64]{0,2,1:T(8,128)(2,1)} %bitcast.70, bf16[256,16,64]{0,2,1:T(8,128)(2,1)} %bitcast.68), kind=kOutput, calls=%fused_computation.43 | convolution fusion | flops 69206272 | bytes 2892032 | tf_op jit(solution)/shard_map/sub | solution.py:29
  56.0 2.2 convolution_convert_fusion.4
  58.2 0.0 copy-done.2
  58.3 0.0 copy-done
  58.3 0.8 fusion.29
  59.0 0.0 copy-done.7
  59.1 1.5 convolution_convert_fusion
  60.6 13.2 %all-to-all-done = bf16[16,32,1024]{2,1,0:T(8,128)(2,1)} async-done(((bf16[16,32,1024]{2,1,0:T(8,128)(2,1)}), bf16[16,32,1024]{2,1,0:T(8,128)(2,1)}, u32[]{:S(2)}, u32[]{:S(2)}) %all-to-all-start) | async-done | bytes 1048608 | tf_op jit(solution)/shard_map/all_to_all | solution.py:90
  73.8 3.7 %all-to-all-start.2 = ((bf16[16,32,1024]{2,1,0:T(8,128)(2,1)}), bf16[16,32,1024]{2,1,0:T(8,128)(2,1)S(1)}, u32[]{:S(2)}, u32[]{:S(2)}) async-start(bf16[16,32,1024]{2,1,0:T(8,128)(2,1)} %bitcast.19), calls=%async_computation.2 | async-start | bytes 2097152 | tf_op jit(solution)/shard_map/all_to_all | solution.py:92
  77.5 1.3 copy.43
  78.8 2.4 %copy.42 = bf16[8,2,32,1024]{3,2,0,1:T(8,128)(2,1)} copy(bf16[8,2,32,1024]{3,2,1,0:T(8,128)(2,1)} %bitcast.10) | data formatting | bytes 2097152 | tf_op jit(solution)/shard_map/all_to_all | solution.py:90
  81.3 22.0 %all-to-all-done.2 = bf16[16,32,1024]{2,1,0:T(8,128)(2,1)S(1)} async-done(((bf16[16,32,1024]{2,1,0:T(8,128)(2,1)}), bf16[16,32,1024]{2,1,0:T(8,128)(2,1)S(1)}, u32[]{:S(2)}, u32[]{:S(2)}) %all-to-all-start.2) | async-done | bytes 1048608 | tf_op jit(solution)/shard_map/all_to_all | solution.py:92
  103.2 1.1 copy.44
  104.3 10.3 %fusion.30 = f32[2,256,2816]{2,1,0:T(8,128)} fusion(bf16[2,256,1024]{2,1,0:T(8,128)(2,1)} %bitcast.65, bf16[2,1024,2816]{1,2,0:T(8,128)(2,1)} %all-gather.3.cloned.1.call-done), kind=kOutput, calls=%fused_computation.45 | convolution fusion | flops 2952790016 | bytes 18350080 | tf_op jit(solution)/shard_map/erd,edf->erf/dot_general | solution.py:43
  114.6 13.8 %fusion.31 = f32[2,256,2816]{2,1,0:T(8,128)} fusion(bf16[2,256,1024]{2,1,0:T(8,128)(2,1)S(1)} %bitcast.63, bf16[2,1024,2816]{1,2,0:T(8,128)(2,1)} %all-gather.3.cloned.1.call-done), kind=kOutput, calls=%fused_computation.46 | convolution fusion | flops 2952790016 | bytes 18350080 | tf_op jit(solution)/shard_map/erd,edf->erf/dot_general | solution.py:44
  128.4 37.1 %all-gather.5.cloned.1.call-done = bf16[2,1024,2816]{1,2,0:T(8,128)(2,1)} async-done(((bf16[2,1024,704]{1,2,0:T(8,128)(2,1)}), bf16[2,1024,2816]{1,2,0:T(8,128)(2,1)}) %all-gather.5.cloned.1.call-update) | async-done | bytes 11534352 | tf_op jit(solution)/shard_map/all_gather | solution.py:99
  165.5 0.0 copy-done.3
  165.5 15.6 %multiply_convert_fusion = bf16[2,256,2816]{2,1,0:T(8,128)(2,1)} fusion(f32[2,256,2816]{2,1,0:T(8,128)} %fusion.30, f32[2,256,2816]{2,1,0:T(8,128)} %fusion.31, bf16[2,256,1024]{2,1,0:T(8,128)(2,1)S(1)} %bitcast.64, bf16[2,1024,2816]{1,2,0:T(8,128)(2,1)} %all-gather.5.cloned.1.call-done), kind=kOutput, calls=%fused_computation.1 | convolution fusion | flops 2970091520 | bytes 27000832 | tf_op jit(solution)/shard_map/erd,edf->erf/dot_general | solution.py:45
  181.1 8.4 %convolution_convert_fusion.3 = bf16[2,256,1024]{2,1,0:T(8,128)(2,1)S(1)} fusion(bf16[2,256,2816]{2,1,0:T(8,128)(2,1)} %multiply_convert_fusion, bf16[2,1024,2816]{1,2,0:T(8,128)(2,1)} %all-gather.3.cloned.1.call-done), kind=kOutput, calls=%fused_computation.12 | convolution fusion | flops 2953314304 | bytes 15466496 | tf_op jit(solution)/shard_map/erf,edf->erd/dot_general | solution.py:49
  189.5 1.1 copy.45
  190.6 31.4 %all_to_all.69 = bf16[2,256,1024]{2,0,1:T(2,128)(2,1)S(1)} all-to-all(bf16[2,256,1024]{2,0,1:T(2,128)(2,1)S(1)} %copy.45), channel_id=1, replica_groups=mesh['expert'=8,'dp'=4] {'expert'}, dimensions={1} | all-to-all | bytes 2097152 | tf_op jit(solution)/shard_map/all_to_all | solution.py:101
  222.1 0.3 copy.46
  222.3 0.1 copy.47
  222.4 1.3 fusion.4
  223.7 0.0 copy-done.1
  (9 shorter events, 0.0 us)
Async XLA Ops:
  6.5 51.7 %copy-start = (bf16[1024,1024]{1,0:T(8,128)(2,1)S(1)}, bf16[1024,1024]{1,0:T(8,128)(2,1)}, u32[]{:S(2)}) copy-start(bf16[1024,1024]{1,0:T(8,128)(2,1)} %param.25) | copy-start | bytes 6291460
  6.5 1.5 copy-start.4
  6.5 1.7 copy-start.8
  6.5 1.7 copy-start.9
  6.5 1.7 copy-start.6
  6.5 97.8 %all-gather.3.cloned.1.call-start = ((), (), s32[]{:S(2)}) async-start(), calls=%async_computation.4 | async-start | bytes 14417920 | tf_op jit(solution)/shard_map/all_gather | solution.py:98
  7.3 41.6 %copy-start.5 = (bf16[1,1,128,1024]{3,2,1,0:T(8,128)(2,1)S(1)}, bf16[1,1,128,1024]{3,2,1,0:T(8,128)(2,1)}, u32[]{:S(2)}) copy-start(bf16[1,1,128,1024]{3,2,1,0:T(8,128)(2,1)} %param.16) | copy-start | bytes 786436
  7.3 158.2 %all-gather.5.cloned.1.call-start = ((), (), s32[]{:S(2)}) async-start(), calls=%async_computation.5 | async-start | bytes 14417920 | tf_op jit(solution)/shard_map/all_gather | solution.py:99
  10.9 33.0 %all-to-all-start.1 = ((bf16[16,32,1024]{2,1,0:T(8,128)(2,1)}), bf16[16,32,1024]{2,1,0:T(8,128)(2,1)S(1)}, u32[]{:S(2)}, u32[]{:S(2)}) async-start(bf16[16,32,1024]{2,1,0:T(8,128)(2,1)} %bitcast.66), calls=%async_computation.1 | async-start | bytes 2097152 | tf_op jit(solution)/shard_map/all_to_all | solution.py:91
  44.0 14.3 %copy-start.2 = (bf16[16,32,1024]{2,1,0:T(8,128)(2,1)}, bf16[16,32,1024]{2,1,0:T(8,128)(2,1)S(1)}, u32[]{:S(2)}) copy-start(bf16[16,32,1024]{2,1,0:T(8,128)(2,1)S(1)} %all-to-all-done.1) | copy-start | bytes 3145732
  44.0 29.8 %all-to-all-start = ((bf16[16,32,1024]{2,1,0:T(8,128)(2,1)}), bf16[16,32,1024]{2,1,0:T(8,128)(2,1)}, u32[]{:S(2)}, u32[]{:S(2)}) async-start(bf16[16,32,1024]{2,1,0:T(8,128)(2,1)} %bitcast.62), calls=%async_computation | async-start | bytes 2097152 | tf_op jit(solution)/shard_map/all_to_all | solution.py:90
  56.0 3.0 %copy-start.7 = (f32[1,1,256]{2,1,0:T(1,128)S(1)}, f32[1,1,256]{2,1,0:T(1,128)}, u32[]{:S(2)}) copy-start(f32[1,1,256]{2,1,0:T(1,128)} %param.21) | copy-start | bytes 3076
  73.8 29.5 %all-to-all-start.2 = ((bf16[16,32,1024]{2,1,0:T(8,128)(2,1)}), bf16[16,32,1024]{2,1,0:T(8,128)(2,1)S(1)}, u32[]{:S(2)}, u32[]{:S(2)}) async-start(bf16[16,32,1024]{2,1,0:T(8,128)(2,1)} %bitcast.19), calls=%async_computation.2 | async-start | bytes 2097152 | tf_op jit(solution)/shard_map/all_to_all | solution.py:92
  114.6 50.9 %copy-start.3 = (bf16[2,8,32,1024]{3,2,1,0:T(8,128)(2,1)S(1)}, bf16[2,8,32,1024]{3,2,1,0:T(8,128)(2,1)}, u32[]{:S(2)}) copy-start(bf16[2,8,32,1024]{3,2,1,0:T(8,128)(2,1)} %copy.44) | copy-start | bytes 3145732
  181.1 42.6 %copy-start.1 = (bf16[1024,1024]{1,0:T(8,128)(2,1)S(1)}, bf16[1024,1024]{1,0:T(8,128)(2,1)}, u32[]{:S(2)}) copy-start(bf16[1024,1024]{1,0:T(8,128)(2,1)} %param.25) | copy-start | bytes 6291460
Sparse Core Ops, SparseCore 0:
  8.9 78.8 all-gather.2
  89.4 76.1 all-gather.4
where the time goes:
time: 231 us
  waiting for transfers between devices  96.8 us (42%)
  matrix products  62.3 us (27%)
  blocking collectives  31.4 us (14%)
  starting transfers between devices  15.3 us (7%)
  between operations  14.2 us (6%)
  local copies, waits for them, and re-layouts  10.3 us (4%)
    all_gather x1, waiting for transfers between devices, body(): lax.all_gather(w_out_t, 'dp', axis=2, tiled=True)  37.1 us
    all_to_all x1, blocking collectives, body(): lax.all_to_all(slot_mult.astype(jnp.bfloat16), 'expert', split_axis=1, co...  31.4 us
    all_to_all x1, waiting for transfers between devices, body(): lax.all_to_all(dispatch(base_inputs), 'expert', split_axis=0, concat_axis...  23.1 us
    all_to_all x1, waiting for transfers between devices, body(): lax.all_to_all(dispatch(scaled_mult), 'expert', split_axis=0, concat_axis...  22 us
    dot_general x1, matrix products, expert_terms(): jnp.einsum('erd,edf->erf', rows_mult, part_out, preferred_element_type=jn...  15.6 us
    dot_general x1, matrix products, expert_terms(): jnp.einsum('erd,edf->erf', rows_base, part_in, preferred_element_type=jnp...  13.8 us
    all_to_all x1, waiting for transfers between devices, body(): lax.all_to_all(dispatch(inputs), 'expert', split_axis=0, concat_axis=1, t...  13.2 us
    dot_general x1, matrix products, expert_terms(): jnp.einsum('erd,edf->erf', rows_in, part_in, preferred_element_type=jnp.f...  10.3 us
  transfers between devices with their start and end apart: 5, of which 4 were waited for; matrix products, arithmetic and copies ran while one was open for 20% of the time, Pallas kernels for 0%

commit v1 on v0

--- a/solution.py
+++ b/solution.py
@@ -96,7 +96,7 @@
         sent_base,
         sent_mult,
         lax.all_gather(w_in, "dp", axis=2, tiled=True),
-        lax.all_gather(w_out_t, "dp", axis=2, tiled=True),
+        jnp.concatenate(lax.all_gather(w_out_t, "dp"), axis=2),
     )
     returned = lax.all_to_all(
         slot_mult.astype(jnp.bfloat16), "expert", split_axis=1, concat_axis=0, tiled=True

time: 231 us -> 259 us (1.12)
  waiting for transfers between devices: 96.8 us -> 111 us
  local copies, waits for them, and re-layouts: 10.3 us -> 20.3 us
  matrix products: 62.3 us -> 65.7 us
    all_gather x1, waiting for transfers between devices: 0.01 us -> 51.1 us  [body(): lax.all_gather(w_in, 'dp', axis=2, tiled=True)]
    all_gather x1, waiting for transfers between devices: 37.1 us -> 0.01 us  [body(): lax.all_gather(w_out_t, 'dp')]
    reshape x0 -> x1, local copies, waits for them, and re-layouts: none -> 10.1 us  [body(): jnp.concatenate(lax.all_gather(w_out_t, 'dp'), axis=2)]
    dot_general x1, matrix products: 10.3 us -> 13.6 us  [expert_terms(): jnp.einsum('erd,edf->erf', rows_in, part_in, preferred_element_type=jnp.f...]
  transfers between devices with their start and end apart: 5 -> 5, of which waited for: 4 -> 4; matrix products, arithmetic and copies ran while one was open for 20% -> 12% of each run, Pallas kernels for 0% -> 0%
where the time goes in v1:
time: 259 us; the launch traced here: 258 us
  waiting for transfers between devices  111 us (43%)
  matrix products  65.7 us (25%)
  blocking collectives  31.4 us (12%)
  local copies, waits for them, and re-layouts  20.3 us (8%)
  starting transfers between devices  15.3 us (6%)
  between operations  14.2 us (5%)
    all_gather x1, waiting for transfers between devices, body(): lax.all_gather(w_in, 'dp', axis=2, tiled=True)  51.1 us
    all_to_all x1, blocking collectives, body(): lax.all_to_all(slot_mult.astype(jnp.bfloat16), 'expert', split_axis=1, co...  31.4 us
    all_to_all x1, waiting for transfers between devices, body(): lax.all_to_all(dispatch(base_inputs), 'expert', split_axis=0, concat_axis...  23.1 us
    all_to_all x1, waiting for transfers between devices, body(): lax.all_to_all(dispatch(scaled_mult), 'expert', split_axis=0, concat_axis...  22 us
    dot_general x1, matrix products, expert_terms(): jnp.einsum('erd,edf->erf', rows_mult, part_out, preferred_element_type=jn...  15.6 us
    dot_general x1, matrix products, expert_terms(): jnp.einsum('erd,edf->erf', rows_base, part_in, preferred_element_type=jnp...  13.8 us
    dot_general x1, matrix products, expert_terms(): jnp.einsum('erd,edf->erf', rows_in, part_in, preferred_element_type=jnp.f...  13.6 us
    all_to_all x1, waiting for transfers between devices, body(): lax.all_to_all(dispatch(inputs), 'expert', split_axis=0, concat_axis=1, t...  13.2 us
  transfers between devices with their start and end apart: 5, of which 4 were waited for; matrix products, arithmetic and copies ran while one was open for 12% of the time, Pallas kernels for 0%

profile of v1, /device:TPU:0, one launch (start us, length us, event | category | flops | bytes accessed | tf_op | source)
XLA Modules:
  0.0 258.0 jit_solution(9522335907243748760)
XLA Ops:
  6.5 0.0 copy-start
  6.5 0.0 copy-start.5
  6.5 0.0 all-gather.6.cloned.1.call-start
  6.6 0.7 all-gather.6.cloned.1.call-update
  7.3 0.0 copy-start.6
  7.3 0.0 all-gather.4.cloned.1.call-start
  7.3 0.7 all-gather.4.cloned.1.call-update
  8.0 0.0 copy-done.5
  8.1 0.2 fusion.5
  8.2 0.0 copy-done.9
  8.3 0.0 copy-done.10
  8.3 0.0 copy-done.7
  8.3 2.6 %convolution_convert_fusion.1 = bf16[512,1024]{1,0:T(8,128)(2,1)} fusion(bf16[1,1,256,1024]{3,2,1,0:T(8,128)(2,1)} %param.14, f32[256]{0:T(256)S(1)} %add_rsqrt_fusion, f32[1024]{0:T(1024)S(1)} %copy-done.7, s32[256]{0:T(256)S(1)} %bitcast.77), kind=kOutput, calls=%fused_computation.10 | convolution fusion | flops 270139392 | bytes 1579008 | tf_op jit(solution)/shard_map/dot_general | solution.py:82
  10.9 7.3 %all-to-all-start.1 = ((bf16[16,32,1024]{2,1,0:T(8,128)(2,1)}), bf16[16,32,1024]{2,1,0:T(8,128)(2,1)S(1)}, u32[]{:S(2)}, u32[]{:S(2)}) async-start(bf16[16,32,1024]{2,1,0:T(8,128)(2,1)} %bitcast.72), calls=%async_computation.1 | async-start | bytes 2097152 | tf_op jit(solution)/shard_map/all_to_all | solution.py:91
  18.2 2.6 %convolution_convert_fusion.2 = bf16[512,1024]{1,0:T(8,128)(2,1)} fusion(bf16[1,1,256,1024]{3,2,1,0:T(8,128)(2,1)} %param.13, f32[256]{0:T(256)S(1)} %add_rsqrt_fusion, f32[1024]{0:T(1024)S(1)} %copy-done.7, s32[256]{0:T(256)S(1)} %bitcast.78), kind=kOutput, calls=%fused_computation.11 | convolution fusion | flops 270139392 | bytes 1579008 | tf_op jit(solution)/shard_map/dot_general | solution.py:82
  20.8 23.1 %all-to-all-done.1 = bf16[16,32,1024]{2,1,0:T(8,128)(2,1)S(1)} async-done(((bf16[16,32,1024]{2,1,0:T(8,128)(2,1)}), bf16[16,32,1024]{2,1,0:T(8,128)(2,1)S(1)}, u32[]{:S(2)}, u32[]{:S(2)}) %all-to-all-start.1) | async-done | bytes 1048608 | tf_op jit(solution)/shard_map/all_to_all | solution.py:91
  44.0 4.2 %all-to-all-start = ((bf16[16,32,1024]{2,1,0:T(8,128)(2,1)}), bf16[16,32,1024]{2,1,0:T(8,128)(2,1)}, u32[]{:S(2)}, u32[]{:S(2)}) async-start(bf16[16,32,1024]{2,1,0:T(8,128)(2,1)} %bitcast.68), calls=%async_computation | async-start | bytes 2097152 | tf_op jit(solution)/shard_map/all_to_all | solution.py:90
  48.9 0.0 copy-done.6
  48.9 0.8 copy.43
  49.7 1.1 copy.45
  50.8 2.0 copy.44
  52.9 3.2 %fusion.28 = (f32[16,128]{1,0:T(8,128)S(1)}, f32[16,128,256]{2,1,0:T(8,128)}) fusion(pred[256]{0:T(512)(128)(4,1)S(1)} %iota_compare_fusion.5, bf16[128,16,64]{0,2,1:T(8,128)(2,1)} %bitcast.76, bf16[256,16,64]{0,2,1:T(8,128)(2,1)} %bitcast.74), kind=kOutput, calls=%fused_computation.43 | convolution fusion | flops 69206272 | bytes 2892032 | tf_op jit(solution)/shard_map/sub | solution.py:29
  56.0 2.2 convolution_convert_fusion.4
  58.2 0.0 copy-done.2
  58.2 0.0 copy-done
  58.3 0.8 fusion.29
  59.0 0.0 copy-done.8
  59.0 1.5 convolution_convert_fusion
  60.6 13.2 %all-to-all-done = bf16[16,32,1024]{2,1,0:T(8,128)(2,1)} async-done(((bf16[16,32,1024]{2,1,0:T(8,128)(2,1)}), bf16[16,32,1024]{2,1,0:T(8,128)(2,1)}, u32[]{:S(2)}, u32[]{:S(2)}) %all-to-all-start) | async-done | bytes 1048608 | tf_op jit(solution)/shard_map/all_to_all | solution.py:90
  73.8 3.7 %all-to-all-start.2 = ((bf16[16,32,1024]{2,1,0:T(8,128)(2,1)}), bf16[16,32,1024]{2,1,0:T(8,128)(2,1)S(1)}, u32[]{:S(2)}, u32[]{:S(2)}) async-start(bf16[16,32,1024]{2,1,0:T(8,128)(2,1)} %bitcast.19), calls=%async_computation.2 | async-start | bytes 2097152 | tf_op jit(solution)/shard_map/all_to_all | solution.py:92
  77.5 1.3 copy.47
  78.8 2.4 copy.46
  81.2 22.0 %all-to-all-done.2 = bf16[16,32,1024]{2,1,0:T(8,128)(2,1)S(1)} async-done(((bf16[16,32,1024]{2,1,0:T(8,128)(2,1)}), bf16[16,32,1024]{2,1,0:T(8,128)(2,1)S(1)}, u32[]{:S(2)}, u32[]{:S(2)}) %all-to-all-start.2) | async-done | bytes 1048608 | tf_op jit(solution)/shard_map/all_to_all | solution.py:92
  103.2 1.1 copy.48
  104.3 10.1 %copy.49 = bf16[2,1024,4,704]{1,3,2,0:T(8,128)(2,1)} copy(bf16[2,1024,4,704]{1,3,0,2:T(8,128)(2,1)} %bitcast.62) | data formatting | bytes 23068672 | tf_op jit(solution)/shard_map/reshape | solution.py:99
  114.4 51.1 %all-gather.4.cloned.1.call-done = bf16[2,1024,2816]{1,2,0:T(8,128)(2,1)} async-done(((bf16[2,1024,704]{1,2,0:T(8,128)(2,1)}), bf16[2,1024,2816]{1,2,0:T(8,128)(2,1)}) %all-gather.4.cloned.1.call-update) | async-done | bytes 11534352 | tf_op jit(solution)/shard_map/all_gather | solution.py:98
  165.5 0.0 copy-done.3
  165.5 13.6 %fusion.30 = f32[2,256,2816]{2,1,0:T(8,128)} fusion(bf16[2,256,1024]{2,1,0:T(8,128)(2,1)S(1)} %bitcast.70, bf16[2,1024,2816]{1,2,0:T(8,128)(2,1)} %all-gather.4.cloned.1.call-done), kind=kOutput, calls=%fused_computation.45 | convolution fusion | flops 2952790016 | bytes 18350080 | tf_op jit(solution)/shard_map/erd,edf->erf/dot_general | solution.py:43
  179.2 13.8 %fusion.31 = f32[2,256,2816]{2,1,0:T(8,128)} fusion(bf16[2,256,1024]{2,1,0:T(8,128)(2,1)S(1)} %bitcast.69, bf16[2,1024,2816]{1,2,0:T(8,128)(2,1)} %all-gather.4.cloned.1.call-done), kind=kOutput, calls=%fused_computation.46 | convolution fusion | flops 2952790016 | bytes 18350080 | tf_op jit(solution)/shard_map/erd,edf->erf/dot_general | solution.py:44
  193.0 0.0 copy-done.4
  193.0 15.6 %multiply_convert_fusion = bf16[2,256,2816]{2,1,0:T(8,128)(2,1)} fusion(f32[2,256,2816]{2,1,0:T(8,128)} %fusion.30, f32[2,256,2816]{2,1,0:T(8,128)} %fusion.31, bf16[2,256,1024]{2,1,0:T(8,128)(2,1)S(1)} %bitcast.71, bf16[2,1024,2816]{1,2,0:T(8,128)(2,1)} %bitcast.63), kind=kOutput, calls=%fused_computation.1 | convolution fusion | flops 2970091520 | bytes 27000832 | tf_op jit(solution)/shard_map/erd,edf->erf/dot_general | solution.py:45
  208.6 8.4 %convolution_convert_fusion.3 = bf16[2,256,1024]{2,1,0:T(8,128)(2,1)S(1)} fusion(bf16[2,256,2816]{2,1,0:T(8,128)(2,1)} %multiply_convert_fusion, bf16[2,1024,2816]{1,2,0:T(8,128)(2,1)} %all-gather.4.cloned.1.call-done), kind=kOutput, calls=%fused_computation.12 | convolution fusion | flops 2953314304 | bytes 15466496 | tf_op jit(solution)/shard_map/erf,edf->erd/dot_general | solution.py:49
  217.0 1.1 copy.51
  218.1 31.4 %all_to_all.69 = bf16[2,256,1024]{2,0,1:T(2,128)(2,1)S(1)} all-to-all(bf16[2,256,1024]{2,0,1:T(2,128)(2,1)S(1)} %copy.51), channel_id=1, replica_groups=mesh['expert'=8,'dp'=4] {'expert'}, dimensions={1} | all-to-all | bytes 2097152 | tf_op jit(solution)/shard_map/all_to_all | solution.py:101
  249.5 0.3 copy.52
  249.8 0.1 copy.53
  249.9 1.3 fusion.4
  251.2 0.0 copy-done.1
  (12 shorter events, 0.0 us)
Async XLA Ops:
  6.5 51.7 %copy-start = (bf16[1024,1024]{1,0:T(8,128)(2,1)S(1)}, bf16[1024,1024]{1,0:T(8,128)(2,1)}, u32[]{:S(2)}) copy-start(bf16[1024,1024]{1,0:T(8,128)(2,1)} %param.25) | copy-start | bytes 6291460
  6.5 1.5 copy-start.5
  6.5 1.7 copy-start.9
  6.5 1.7 copy-start.10
  6.5 1.7 copy-start.7
  6.5 97.7 %all-gather.6.cloned.1.call-start = ((), (), s32[]{:S(2)}) async-start(), calls=%async_computation.5 | async-start | bytes 14417920 | tf_op jit(solution)/shard_map/all_gather | solution.py:99
  7.3 41.6 %copy-start.6 = (bf16[1,1,128,1024]{3,2,1,0:T(8,128)(2,1)S(1)}, bf16[1,1,128,1024]{3,2,1,0:T(8,128)(2,1)}, u32[]{:S(2)}) copy-start(bf16[1,1,128,1024]{3,2,1,0:T(8,128)(2,1)} %param.16) | copy-start | bytes 786436
  7.3 158.2 %all-gather.4.cloned.1.call-start = ((), (), s32[]{:S(2)}) async-start(), calls=%async_computation.4 | async-start | bytes 14417920 | tf_op jit(solution)/shard_map/all_gather | solution.py:98
  10.9 33.0 %all-to-all-start.1 = ((bf16[16,32,1024]{2,1,0:T(8,128)(2,1)}), bf16[16,32,1024]{2,1,0:T(8,128)(2,1)S(1)}, u32[]{:S(2)}, u32[]{:S(2)}) async-start(bf16[16,32,1024]{2,1,0:T(8,128)(2,1)} %bitcast.72), calls=%async_computation.1 | async-start | bytes 2097152 | tf_op jit(solution)/shard_map/all_to_all | solution.py:91
  44.0 14.3 %copy-start.2 = (bf16[16,32,1024]{2,1,0:T(8,128)(2,1)}, bf16[16,32,1024]{2,1,0:T(8,128)(2,1)S(1)}, u32[]{:S(2)}) copy-start(bf16[16,32,1024]{2,1,0:T(8,128)(2,1)S(1)} %all-to-all-done.1) | copy-start | bytes 3145732
  44.0 29.8 %all-to-all-start = ((bf16[16,32,1024]{2,1,0:T(8,128)(2,1)}), bf16[16,32,1024]{2,1,0:T(8,128)(2,1)}, u32[]{:S(2)}, u32[]{:S(2)}) async-start(bf16[16,32,1024]{2,1,0:T(8,128)(2,1)} %bitcast.68), calls=%async_computation | async-start | bytes 2097152 | tf_op jit(solution)/shard_map/all_to_all | solution.py:90
  56.0 3.0 %copy-start.8 = (f32[1,1,256]{2,1,0:T(1,128)S(1)}, f32[1,1,256]{2,1,0:T(1,128)}, u32[]{:S(2)}) copy-start(f32[1,1,256]{2,1,0:T(1,128)} %param.21) | copy-start | bytes 3076
  73.8 29.5 %all-to-all-start.2 = ((bf16[16,32,1024]{2,1,0:T(8,128)(2,1)}), bf16[16,32,1024]{2,1,0:T(8,128)(2,1)S(1)}, u32[]{:S(2)}, u32[]{:S(2)}) async-start(bf16[16,32,1024]{2,1,0:T(8,128)(2,1)} %bitcast.19), calls=%async_computation.2 | async-start | bytes 2097152 | tf_op jit(solution)/shard_map/all_to_all | solution.py:92
  104.3 61.2 %copy-start.3 = (bf16[8,2,32,1024]{3,2,0,1:T(8,128)(2,1)S(1)}, bf16[8,2,32,1024]{3,2,0,1:T(8,128)(2,1)}, u32[]{:S(2)}) copy-start(bf16[8,2,32,1024]{3,2,0,1:T(8,128)(2,1)} %copy.46) | copy-start | bytes 3145732
  179.2 13.8 %copy-start.4 = (bf16[2,8,32,1024]{3,2,1,0:T(8,128)(2,1)S(1)}, bf16[2,8,32,1024]{3,2,1,0:T(8,128)(2,1)}, u32[]{:S(2)}) copy-start(bf16[2,8,32,1024]{3,2,1,0:T(8,128)(2,1)} %copy.48) | copy-start | bytes 3145732
  208.6 42.6 %copy-start.1 = (bf16[1024,1024]{1,0:T(8,128)(2,1)S(1)}, bf16[1024,1024]{1,0:T(8,128)(2,1)}, u32[]{:S(2)}) copy-start(bf16[1024,1024]{1,0:T(8,128)(2,1)} %param.25) | copy-start | bytes 6291460
Sparse Core Ops, SparseCore 0:
  8.9 78.8 all-gather.5
  89.4 76.1 all-gather.3
